TPU v7x, 32 devices: a whole 2x2x4 slice. The times are simulated.
32 devices in a mesh: grp: 4 (over y, core), dev: 8 (over z, x).
Axes of the slice: x: 2, y: 2, z: 4, core: 2. Of those that a mesh axis runs over, the one named last changes fastest.
Arguments:
- train_grads: bfloat16 [4096, 1024], P(('grp', 'dev')), may hold values from -192 to 192, as said below
- queries: bfloat16 [512, 1024], P('grp'), may hold values from -6 to 6
Outputs:
- scores: bfloat16 [4096, 512], P(('grp', 'dev'))
Inputs may be any that keep to these rules, and one draw needn't show every extreme that they name: `train_grads`: Real-valued projected gradients whose columns and rows differ in scale.
All inputs are finite; a program needn't handle non-finite values. Where the computation divides by a largest or mean magnitude, that divisor is 1e-20 or more.
Results may differ from a plain program's by a relative error of at most 0.001.
The roundings to bfloat16 on the way count: a program that leaves them out, or rounds other values in their place, can miss the bound.
Values may be sent and summed in bfloat16 or wider, within the bound.
No kernel may reach another device: no remote copies, remote signals or barrier semaphores. Data moves between devices by JAX's collectives and lax.ppermute only.
A program may use at most 64 MiB of HBM per device.

v0:
```python
import jax
import jax.numpy as jnp
from jax import lax
from jax.sharding import PartitionSpec as P

ITERS = 8
damping_ratio = 0.1


def local_solve(gram, own, total, width):
    normed = gram / total
    damp = damping_ratio * jnp.trace(gram) / (total * width)
    bound = jnp.max(jnp.sum(jnp.abs(normed), axis=1)) + damp
    step = 1.0 / bound
    oper = normed + damp * jnp.eye(width, dtype=jnp.float32)
    state = step * own
    for index in range(ITERS):
        state = state + step * (own - jnp.dot(state, oper, precision=lax.Precision.HIGHEST))
    return state.astype(jnp.bfloat16)


def body(train_grads, queries):
    rows, width = train_grads.shape
    ndevice = lax.axis_size("dev")
    total = rows * ndevice * lax.axis_size("grp")
    qvals = queries.astype(jnp.float32)
    qrows = qvals.shape[0] // ndevice
    qstart = lax.axis_index("dev") * qrows
    own = lax.dynamic_slice_in_dim(qvals, qstart, qrows, 0)
    gram = lax.psum(
        lax.dot_general(
            train_grads, train_grads, (((0,), (0,)), ((), ())), preferred_element_type=jnp.float32
        ),
        ("grp", "dev"),
    )
    mine = local_solve(gram, own, total, width)
    prepared = lax.all_gather(mine, "dev", axis=0, tiled=True)
    return lax.dot_general(
        train_grads,
        lax.all_gather(prepared, "grp", axis=0, tiled=True),
        (((1,), (1,)), ((), ())),
        preferred_element_type=jnp.float32,
    ).astype(jnp.bfloat16)


def solution(mesh):
    return jax.shard_map(
        body,
        mesh=mesh,
        in_specs=(P(("grp", "dev"), None), P("grp", None)),
        out_specs=P(("grp", "dev"), None),
        check_vma=False,
    )
```

profile of v0, /device:TPU:0, one launch (start us, length us, event | category | flops | bytes accessed | tf_op | source)
XLA Modules:
  0.0 242.2 jit_solution(13720680544935687470)
XLA Ops:
  6.5 0.0 all-reduce.2.cloned.1.call-start
  6.5 0.9 copy-done
  7.5 2.7 %fusion.21 = f32[1024,1024]{1,0:T(8,128)} fusion(bf16[128,1024]{1,0:T(8,128)(2,1)S(1)} %copy-done), kind=kOutput, calls=%fused_computation.35 | convolution fusion | flops 268435456 | bytes 4456448 | tf_op jit(solution)/shard_map/dot_general | solution.py:31
  10.2 0.0 all-reduce.2.cloned.1.call-update
  10.2 0.0 all-gather.2.cloned.1.call-start
  10.3 147.6 %all-reduce.2.cloned.1.call-done = f32[1024,1024]{1,0:T(8,128)} async-done(((f32[1024,1024]{1,0:T(8,128)}), f32[1024,1024]{1,0:T(8,128)}) %all-reduce.2.cloned.1.call-update) | async-done | bytes 4194320 | tf_op jit(solution)/shard_map/psum | solution.py:30
  157.9 3.3 %select_reduce_fusion = (f32[]{:T(128)}, f32[1024]{0:T(1024)S(1)}) fusion(f32[1024,1024]{1,0:T(8,128)} %all-reduce.2.cloned.1.call-done), kind=kLoop, calls=%fused_computation.1 | loop fusion | flops 6290431 | bytes 4198404 | tf_op jit(solution)/shard_map/jit(trace)/reduce_sum | solution.py:12
  161.9 0.6 reduce_max.9
  163.2 0.0 copy-done.2
  163.2 0.0 copy-start.1
  163.2 4.6 %fusion.2 = f32[16,1024]{1,0:T(8,128)S(1)} fusion(f32[]{:T(128)S(6)} %div.15, bf16[128,1024]{1,0:T(8,128)(2,1)S(1)} %copy-done.2, s32[]{:T(128)S(6)} %select_n.9, f32[1024,1024]{1,0:T(8,128)} %all-reduce.2.cloned.1.call-done, f32[]{:T(128)S(6)} %div.14), kind=kOutput, calls=%fused_computation.15 | convolution fusion | flops 205635584 | bytes 4327936 | tf_op jit(solution)/shard_map/dot_general | solution.py:18
  167.8 0.0 copy-done.1
  167.8 2.3 fusion.4
  170.1 2.3 fusion.6
  172.3 2.3 fusion.8
  174.6 2.3 fusion.10
  176.8 2.4 %fusion.12 = f32[16,1024]{1,0:T(8,128)S(1)} fusion(f32[16,1024]{1,0:T(8,128)S(1)} %fusion.10, f32[]{:T(128)S(6)} %div.15, bf16[128,1024]{1,0:T(8,128)(2,1)S(1)} %copy-done.2, s32[]{:T(128)S(6)} %select_n.9, f32[1024,1024]{1,0:T(8,128)S(1)} %copy-done.1, f32[]{:T(128)S(6)} %div.14), kind=kOutput, calls=%fused_computation.25 | convolution fusion | flops 205586432 | bytes 4423692 | tf_op jit(solution)/shard_map/dot_general | solution.py:18
  179.3 2.3 fusion.14
  181.5 2.3 fusion.17
  183.8 32.8 %all_gather.6 = bf16[128,1024]{1,0:T(8,128)(2,1)} all-gather(bf16[16,1024]{1,0:T(8,128)(2,1)S(1)} %fusion.17), channel_id=1, replica_groups=mesh['grp'=4,'dev'=8] {'dev'}, dimensions={0}, use_global_device_ids=true | all-gather | bytes 294912 | tf_op jit(solution)/shard_map/all_gather | solution.py:37
  216.6 0.0 all-gather.2.cloned.1.call-update
  216.7 16.3 %all-gather.2.cloned.1.call-done = bf16[512,1024]{1,0:T(8,128)(2,1)} async-done(((bf16[128,1024]{1,0:T(8,128)(2,1)}), bf16[512,1024]{1,0:T(8,128)(2,1)}) %all-gather.2.cloned.1.call-update) | async-done | bytes 1048592 | tf_op jit(solution)/shard_map/all_gather | solution.py:40
  233.0 1.7 fusion
  234.6 0.8 copy.3
  (2 shorter events, 0.0 us)
Async XLA Ops:
  6.5 1.0 copy-start
  6.5 151.4 %all-reduce.2.cloned.1.call-start = ((), (), s32[]{:S(2)}) async-start(), calls=%async_computation | async-start | bytes 8388608 | tf_op jit(solution)/shard_map/psum | solution.py:30
  10.2 153.0 %copy-start.2 = (bf16[128,1024]{1,0:T(8,128)(2,1)S(1)}, bf16[128,1024]{1,0:T(8,128)(2,1)}, u32[]{:S(2)}) copy-start(bf16[128,1024]{1,0:T(8,128)(2,1)} %param.3) | copy-start | bytes 786436
  10.2 222.8 %all-gather.2.cloned.1.call-start = ((), (), s32[]{:S(2)}) async-start(), calls=%async_computation.1 | async-start | bytes 1310720 | tf_op jit(solution)/shard_map/all_gather | solution.py:40
  163.2 4.6 %copy-start.1 = (f32[1024,1024]{1,0:T(8,128)S(1)}, f32[1024,1024]{1,0:T(8,128)}, u32[]{:S(2)}) copy-start(f32[1024,1024]{1,0:T(8,128)} %all-reduce.2.cloned.1.call-done) | copy-start | bytes 12582916
Sparse Core Ops, SparseCore 0:
  12.9 144.9 all-reduce.1
  216.8 16.1 all-gather.1
where the time goes:
time: 242 us
  waiting for transfers between devices  164 us (68%)
  blocking collectives  32.8 us (14%)
  matrix products  24.9 us (10%)
  between operations  14.8 us (6%)
  other arithmetic  3.94 us (2%)
    psum x1, waiting for transfers between devices, body(): lax.psum(lax.dot_general(train_grads, train_grads, (((0,), (0,)), ((), ()...  148 us
    all_gather x1, blocking collectives, body(): prepared = lax.all_gather(mine, 'dev', axis=0, tiled=True)  32.8 us
    dot_general x8, matrix products, local_solve(): jnp.dot(state, oper, precision=lax.Precision.HIGHEST)  20.5 us
    all_gather x1, waiting for transfers between devices, body(): lax.all_gather(prepared, 'grp', axis=0, tiled=True)  16.3 us
  transfers between devices with their start and end apart: 2, of which 2 were waited for; matrix products, arithmetic and copies ran while one was open for 0% of the time, Pallas kernels for 0%

commit v1 on v0

--- a/solution.py
+++ b/solution.py
@@ -34,7 +34,9 @@
         ("grp", "dev"),
     )
     mine = local_solve(gram, own, total, width)
-    prepared = lax.all_gather(mine, "dev", axis=0, tiled=True)
+    prepared = jnp.concatenate(
+        lax.all_to_all(jnp.stack([mine] * lax.axis_size("dev")), "dev", 0, 0), axis=0
+    )
     return lax.dot_general(
         train_grads,
         lax.all_gather(prepared, "grp", axis=0, tiled=True),

time: 242 us -> 221 us (0.913)
  blocking collectives: 32.8 us -> 11.8 us
    all_gather x1 -> x0, blocking collectives: 32.8 us -> none  [body(): prepared = lax.all_gather(mine, 'dev', axis=0, tiled=True)]
    all_to_all x0 -> x1, blocking collectives: none -> 11.8 us  [body(): lax.all_to_all(jnp.stack([mine] * lax.axis_size('dev')), 'dev', 0, 0)]
where the time goes in v1:
time: 221 us; the launch traced here: 220 us
  waiting for transfers between devices  163 us (74%)
  matrix products  24.9 us (11%)
  between operations  14.8 us (7%)
  blocking collectives  11.8 us (5%)
  other arithmetic  3.94 us (2%)
    psum x1, waiting for transfers between devices, body(): lax.psum(lax.dot_general(train_grads, train_grads, (((0,), (0,)), ((), ()...  148 us
    dot_general x8, matrix products, local_solve(): jnp.dot(state, oper, precision=lax.Precision.HIGHEST)  20.5 us
    all_gather x1, waiting for transfers between devices, body(): lax.all_gather(prepared, 'grp', axis=0, tiled=True)  15.3 us
    all_to_all x1, blocking collectives, body(): lax.all_to_all(jnp.stack([mine] * lax.axis_size('dev')), 'dev', 0, 0)  11.8 us
  transfers between devices with their start and end apart: 2, of which 2 were waited for; matrix products, arithmetic and copies ran while one was open for 0% of the time, Pallas kernels for 0%

profile of v1, /device:TPU:0, one launch (start us, length us, event | category | flops | bytes accessed | tf_op | source)
XLA Modules:
  0.0 220.3 jit_solution(15454420597564546589)
XLA Ops:
  6.5 0.0 all-reduce.2.cloned.1.call-start
  6.5 0.9 copy-done
  7.5 2.7 %fusion.21 = f32[1024,1024]{1,0:T(8,128)} fusion(bf16[128,1024]{1,0:T(8,128)(2,1)S(1)} %copy-done), kind=kOutput, calls=%fused_computation.35 | convolution fusion | flops 268435456 | bytes 4456448 | tf_op jit(solution)/shard_map/dot_general | solution.py:31
  10.2 0.0 all-reduce.2.cloned.1.call-update
  10.2 0.0 all-gather.2.cloned.1.call-start
  10.3 147.6 %all-reduce.2.cloned.1.call-done = f32[1024,1024]{1,0:T(8,128)} async-done(((f32[1024,1024]{1,0:T(8,128)}), f32[1024,1024]{1,0:T(8,128)}) %all-reduce.2.cloned.1.call-update) | async-done | bytes 4194320 | tf_op jit(solution)/shard_map/psum | solution.py:30
  157.9 3.3 %select_reduce_fusion = (f32[]{:T(128)}, f32[1024]{0:T(1024)S(1)}) fusion(f32[1024,1024]{1,0:T(8,128)} %all-reduce.2.cloned.1.call-done), kind=kLoop, calls=%fused_computation.1 | loop fusion | flops 6290431 | bytes 4198404 | tf_op jit(solution)/shard_map/jit(trace)/reduce_sum | solution.py:12
  161.9 0.6 reduce_max.9
  163.2 0.0 copy-done.2
  163.2 0.0 copy-start.1
  163.2 4.6 %fusion.2 = f32[16,1024]{1,0:T(8,128)S(1)} fusion(f32[]{:T(128)S(6)} %div.15, bf16[128,1024]{1,0:T(8,128)(2,1)S(1)} %copy-done.2, s32[]{:T(128)S(6)} %select_n.9, f32[1024,1024]{1,0:T(8,128)} %all-reduce.2.cloned.1.call-done, f32[]{:T(128)S(6)} %div.14), kind=kOutput, calls=%fused_computation.15 | convolution fusion | flops 205635584 | bytes 4327936 | tf_op jit(solution)/shard_map/dot_general | solution.py:18
  167.8 0.0 copy-done.1
  167.8 2.3 %fusion.4 = f32[16,1024]{1,0:T(8,128)S(1)} fusion(f32[16,1024]{1,0:T(8,128)S(1)} %fusion.2, f32[]{:T(128)S(6)} %div.15, bf16[128,1024]{1,0:T(8,128)(2,1)S(1)} %copy-done.2, s32[]{:T(128)S(6)} %select_n.9, f32[1024,1024]{1,0:T(8,128)S(1)} %copy-done.1, f32[]{:T(128)S(6)} %div.14), kind=kOutput, calls=%fused_computation.17 | convolution fusion | flops 205586432 | bytes 4423692 | tf_op jit(solution)/shard_map/dot_general | solution.py:18
  170.1 2.3 %fusion.6 = f32[16,1024]{1,0:T(8,128)S(1)} fusion(f32[16,1024]{1,0:T(8,128)S(1)} %fusion.4, f32[]{:T(128)S(6)} %div.15, bf16[128,1024]{1,0:T(8,128)(2,1)S(1)} %copy-done.2, s32[]{:T(128)S(6)} %select_n.9, f32[1024,1024]{1,0:T(8,128)S(1)} %copy-done.1, f32[]{:T(128)S(6)} %div.14), kind=kOutput, calls=%fused_computation.19 | convolution fusion | flops 205586432 | bytes 4423692 | tf_op jit(solution)/shard_map/dot_general | solution.py:18
  172.3 2.3 %fusion.8 = f32[16,1024]{1,0:T(8,128)S(1)} fusion(f32[16,1024]{1,0:T(8,128)S(1)} %fusion.6, f32[]{:T(128)S(6)} %div.15, bf16[128,1024]{1,0:T(8,128)(2,1)S(1)} %copy-done.2, s32[]{:T(128)S(6)} %select_n.9, f32[1024,1024]{1,0:T(8,128)S(1)} %copy-done.1, f32[]{:T(128)S(6)} %div.14), kind=kOutput, calls=%fused_computation.21 | convolution fusion | flops 205586432 | bytes 4423692 | tf_op jit(solution)/shard_map/dot_general | solution.py:18
  174.6 2.3 %fusion.10 = f32[16,1024]{1,0:T(8,128)S(1)} fusion(f32[16,1024]{1,0:T(8,128)S(1)} %fusion.8, f32[]{:T(128)S(6)} %div.15, bf16[128,1024]{1,0:T(8,128)(2,1)S(1)} %copy-done.2, s32[]{:T(128)S(6)} %select_n.9, f32[1024,1024]{1,0:T(8,128)S(1)} %copy-done.1, f32[]{:T(128)S(6)} %div.14), kind=kOutput, calls=%fused_computation.23 | convolution fusion | flops 205586432 | bytes 4423692 | tf_op jit(solution)/shard_map/dot_general | solution.py:18
  176.8 2.4 %fusion.12 = f32[16,1024]{1,0:T(8,128)S(1)} fusion(f32[16,1024]{1,0:T(8,128)S(1)} %fusion.10, f32[]{:T(128)S(6)} %div.15, bf16[128,1024]{1,0:T(8,128)(2,1)S(1)} %copy-done.2, s32[]{:T(128)S(6)} %select_n.9, f32[1024,1024]{1,0:T(8,128)S(1)} %copy-done.1, f32[]{:T(128)S(6)} %div.14), kind=kOutput, calls=%fused_computation.25 | convolution fusion | flops 205586432 | bytes 4423692 | tf_op jit(solution)/shard_map/dot_general | solution.py:18
  179.3 2.3 %fusion.14 = f32[16,1024]{1,0:T(8,128)S(1)} fusion(f32[16,1024]{1,0:T(8,128)S(1)} %fusion.12, f32[]{:T(128)S(6)} %div.15, bf16[128,1024]{1,0:T(8,128)(2,1)S(1)} %copy-done.2, s32[]{:T(128)S(6)} %select_n.9, f32[1024,1024]{1,0:T(8,128)S(1)} %copy-done.1, f32[]{:T(128)S(6)} %div.14), kind=kOutput, calls=%fused_computation.27 | convolution fusion | flops 205586432 | bytes 4423692 | tf_op jit(solution)/shard_map/dot_general | solution.py:18
  181.5 2.3 %fusion.17 = bf16[16,1024]{1,0:T(8,128)(2,1)S(1)} fusion(f32[16,1024]{1,0:T(8,128)S(1)} %fusion.14, f32[]{:T(128)S(6)} %div.15, bf16[128,1024]{1,0:T(8,128)(2,1)S(1)} %copy-done.2, s32[]{:T(128)S(6)} %select_n.9, f32[1024,1024]{1,0:T(8,128)S(1)} %copy-done.1, f32[]{:T(128)S(6)} %div.14), kind=kOutput, calls=%fused_computation.30 | convolution fusion | flops 205602816 | bytes 4390924 | tf_op jit(solution)/shard_map/dot_general | solution.py:18
  183.8 11.8 %all_to_all.5 = bf16[8,16,1024]{2,1,0:T(8,128)(2,1)} all-to-all(bf16[8,16,1024]{2,1,0:T(8,128)(2,1)S(1)} %stack.2), channel_id=1, replica_groups=mesh['grp'=4,'dev'=8] {'dev'}, dimensions={0} | all-to-all | bytes 524288 | tf_op jit(solution)/shard_map/all_to_all | solution.py:38
  195.7 0.0 all-gather.2.cloned.1.call-update
  195.7 15.3 %all-gather.2.cloned.1.call-done = bf16[512,1024]{1,0:T(8,128)(2,1)} async-done(((bf16[128,1024]{1,0:T(8,128)(2,1)}), bf16[512,1024]{1,0:T(8,128)(2,1)}) %all-gather.2.cloned.1.call-update) | async-done | bytes 1048592 | tf_op jit(solution)/shard_map/all_gather | solution.py:42
  211.0 1.7 fusion
  212.7 0.8 copy.3
  (3 shorter events, 0.0 us)
Async XLA Ops:
  6.5 1.0 copy-start
  6.5 151.4 %all-reduce.2.cloned.1.call-start = ((), (), s32[]{:S(2)}) async-start(), calls=%async_computation.1 | async-start | bytes 8388608 | tf_op jit(solution)/shard_map/psum | solution.py:30
  10.2 153.0 %copy-start.2 = (bf16[128,1024]{1,0:T(8,128)(2,1)S(1)}, bf16[128,1024]{1,0:T(8,128)(2,1)}, u32[]{:S(2)}) copy-start(bf16[128,1024]{1,0:T(8,128)(2,1)} %param.3) | copy-start | bytes 786436
  10.2 200.8 %all-gather.2.cloned.1.call-start = ((), (), s32[]{:S(2)}) async-start(), calls=%async_computation.2 | async-start | bytes 1310720 | tf_op jit(solution)/shard_map/all_gather | solution.py:42
  163.2 4.6 %copy-start.1 = (f32[1024,1024]{1,0:T(8,128)S(1)}, f32[1024,1024]{1,0:T(8,128)}, u32[]{:S(2)}) copy-start(f32[1024,1024]{1,0:T(8,128)} %all-reduce.2.cloned.1.call-done) | copy-start | bytes 12582916
Sparse Core Ops, SparseCore 0:
  12.9 144.9 all-reduce.1
  195.8 15.1 all-gather.1
